TPU v7x, 32 devices: a whole 2x2x4 slice. The times are simulated.
32 devices in a mesh: fsdp: 2 (over x), ctx: 4 (over y, core), tp: 4 (over z).
Axes of the slice: x: 2, y: 2, z: 4, core: 2. Of those that a mesh axis runs over, the one named last changes fastest.
Arguments:
- block_in: bfloat16 [8, 1024, 2048], P('fsdp', 'ctx', 'tp'), may hold values from -6 to 6
- seg_ids: int32 [8, 1024], P('fsdp'), may hold values from 0 to 7, never falling along the last dimension, each value on 1 to 512 neighbouring positions
- out_cot: bfloat16 [8, 1024, 2048], P('fsdp', 'ctx'), may hold values from -6 to 6
- norm_gain: bfloat16 [2048], P('tp'), may hold values from 0.099609375 to 1.8984375
- mid_gain: bfloat16 [2048], P('tp'), may hold values from 0.099609375 to 1.8984375
- gelu_proj: bfloat16 [2048, 2816], P(('fsdp', 'ctx'), 'tp'), may hold values from -0.125 to 0.125
- scan_proj: bfloat16 [2048, 2816], P(('fsdp', 'ctx'), 'tp'), may hold values from -0.125 to 0.125
- out_proj: bfloat16 [2816, 2048], P('tp', ('fsdp', 'ctx')), may hold values from -0.4375 to 0.4375
- gate_proj: bfloat16 [2048, 6144], P(('fsdp', 'ctx'), 'tp'), may hold values from -0.125 to 0.125
- up_proj: bfloat16 [2048, 6144], P(('fsdp', 'ctx'), 'tp'), may hold values from -0.125 to 0.125
- down_proj: bfloat16 [6144, 2048], P('tp', ('fsdp', 'ctx')), may hold values from -0.109375 to 0.109375
- conv_kernel: float32 [4, 2816], P(None, 'tp'), may hold values from -3 to 3
- conv_bias: float32 [2816], P('tp'), may hold values from -3 to 3
- rate_gate: bfloat16 [16, 176, 176], P('tp'), may hold values from -0.4375 to 0.4375
- input_gate: bfloat16 [16, 176, 176], P('tp'), may hold values from -0.4375 to 0.4375
- rate_bias: float32 [2816], P('tp'), may hold values from -4 to 4
- input_bias: float32 [2816], P('tp'), may hold values from -4 to 4
- decay_param: float32 [2816], P('tp'), may hold values from -16 to -4
Outputs:
- block_out: bfloat16 [8, 1024, 2048], P('fsdp', 'ctx', 'tp')
- grad_in: float32 [8, 1024, 2048], P('fsdp', 'ctx', 'tp')
- grad_norm_gain: float32 [2048], P('tp')
- grad_mid_gain: float32 [2048], P('tp')
- grad_gelu_proj: float32 [2048, 2816], P(('fsdp', 'ctx'), 'tp')
- grad_scan_proj: float32 [2048, 2816], P(('fsdp', 'ctx'), 'tp')
- grad_out_proj: float32 [2816, 2048], P('tp', ('fsdp', 'ctx'))
- grad_gate_proj: float32 [2048, 6144], P(('fsdp', 'ctx'), 'tp')
- grad_up_proj: float32 [2048, 6144], P(('fsdp', 'ctx'), 'tp')
- grad_down_proj: float32 [6144, 2048], P('tp', ('fsdp', 'ctx'))
- grad_conv_kernel: float32 [4, 2816], P(None, 'tp')
- grad_conv_bias: float32 [2816], P('tp')
- grad_rate_gate: float32 [16, 176, 176], P('tp')
- grad_input_gate: float32 [16, 176, 176], P('tp')
- grad_rate_bias: float32 [2816], P('tp')
- grad_input_bias: float32 [2816], P('tp')
- grad_decay_param: float32 [2816], P('tp')
Inputs may be any that keep to these rules, and one draw needn't show every extreme that they name: `seg_ids`: in every row the document numbers never fall; each of the 8 documents covers 1 to 512 positions, and one covers exactly 512.
All inputs are finite; a program needn't handle non-finite values.
Results may differ from a plain program's by a relative error of at most 0.0095.
Values may be sent and summed in bfloat16 or wider, within the bound.
A program may use at most 320 MiB of HBM per device.

v0:
```python
import jax
import jax.numpy as jnp
from jax import lax
from jax.sharding import PartitionSpec as P

CONV = 4
eps_norm = 1e-06


def from_behind(value, axis, steps):
    count = lax.axis_size(axis)
    leading, last = (max(0, -steps), min(count, count - steps))
    return lax.ppermute(value, axis, [(source, source + steps) for source in range(leading, last)])


def entering(value, axis, join, neutral, backward):
    count, mine = (lax.axis_size(axis), lax.axis_index(axis))
    pieces = jax.tree.map(lambda part: lax.all_gather(part, axis), value)
    if backward:
        pieces = jax.tree.map(lambda part: part[::-1], pieces)
        mine = count - 1 - mine
    total = jax.tree.map(
        lambda part, zero: jnp.full_like(part, 0) + jnp.asarray(zero, part.dtype), value, neutral
    )

    def step(position, total):
        longer = join(total, jax.tree.map(lambda part: part[position], pieces))
        return jax.tree.map(lambda new, old: jnp.where(position < mine, new, old), longer, total)

    return lax.fori_loop(0, count - 1, step, total)


def rms_scale(values, gain_vec):
    return (
        values * lax.rsqrt(jnp.mean(values * values, axis=-1, keepdims=True) + eps_norm) * gain_vec
    )


def gelu_tanh(values):
    return jax.nn.gelu(values, approximate=True)


def gate_values(pre_rate, pre_input, decay_param):
    rate_vals = jax.nn.sigmoid(pre_rate)
    input_vals = jax.nn.sigmoid(pre_input)
    log_a = -8.0 * jax.nn.softplus(decay_param) * rate_vals
    return (jnp.exp(log_a), jnp.sqrt(-jnp.expm1(2.0 * log_a)) * input_vals)


def combine(first_part, second_part):
    return (first_part[0] * second_part[0], second_part[0] * first_part[1] + second_part[1])


def matmul(left, right):
    return jnp.dot(left, right, preferred_element_type=jnp.float32)


def matmul_rt(left, right):
    return lax.dot_general(
        left, right, (((1,), (1,)), ((), ())), preferred_element_type=jnp.float32
    )


def matmul_lt(left, right):
    return lax.dot_general(
        left, right, (((0,), (0,)), ((), ())), preferred_element_type=jnp.float32
    )


def shards(
    block_in,
    seg_ids,
    out_cot,
    norm_gain,
    mid_gain,
    gelu_proj,
    scan_proj,
    out_proj,
    gate_proj,
    up_proj,
    down_proj,
    conv_kernel,
    conv_bias,
    rate_gate,
    input_gate,
    rate_bias,
    input_bias,
    decay_param,
):
    seq_count, tok_count, part_width = block_in.shape
    row_count = seq_count * tok_count
    full_in, gain_one, gain_two = (
        lax.all_gather(block_in, "tp", axis=2, tiled=True),
        lax.all_gather(norm_gain, "tp", axis=0, tiled=True),
        lax.all_gather(mid_gain, "tp", axis=0, tiled=True),
    )
    w_gelu, w_scan, w_out, w_gate, w_up, w_down = (
        lax.all_gather(gelu_proj, ("fsdp", "ctx"), axis=0, tiled=True),
        lax.all_gather(scan_proj, ("fsdp", "ctx"), axis=0, tiled=True),
        lax.all_gather(out_proj, ("fsdp", "ctx"), axis=1, tiled=True),
        lax.all_gather(gate_proj, ("fsdp", "ctx"), axis=0, tiled=True),
        lax.all_gather(up_proj, ("fsdp", "ctx"), axis=0, tiled=True),
        lax.all_gather(down_proj, ("fsdp", "ctx"), axis=1, tiled=True),
    )
    full_width = full_in.shape[2]
    rec_width = w_gelu.shape[1]
    head_count = rate_gate.shape[0]
    head_size = rate_gate.shape[1]
    x_rows = full_in.reshape(row_count, full_width).astype(jnp.float32)
    normed_f, norm_one_back = jax.vjp(rms_scale, x_rows, gain_one.astype(jnp.float32))
    normed = normed_f.astype(jnp.bfloat16)
    y_pre = matmul(normed, w_gelu)
    y_act, y_back = jax.vjp(gelu_tanh, y_pre)
    x_branch = matmul(normed, w_scan).astype(jnp.bfloat16).reshape(seq_count, tok_count, rec_width)
    margin_len = CONV - 1
    start_tok = lax.axis_index("ctx") * tok_count
    padded_ids = jnp.concatenate(
        [
            jnp.full((seq_count, margin_len), -1, jnp.int32),
            seg_ids,
            jnp.full((seq_count, margin_len), -2, jnp.int32),
        ],
        axis=1,
    )
    window_ids = lax.dynamic_slice_in_dim(padded_ids, start_tok, tok_count + 2 * margin_len, 1)
    own_ids = window_ids[:, margin_len : margin_len + tok_count]
    back_masks = [
        (window_ids[:, margin_len - offset : margin_len - offset + tok_count] == own_ids).astype(
            jnp.float32
        )[..., None]
        for offset in range(CONV)
    ]
    ahead_masks = [
        (window_ids[:, margin_len + offset : margin_len + offset + tok_count] == own_ids).astype(
            jnp.float32
        )[..., None]
        for offset in range(CONV)
    ]
    prev_edge = from_behind(x_branch[:, tok_count - margin_len :, :], "ctx", 1)
    ext_x = jnp.concatenate([prev_edge, x_branch], axis=1)
    conv_sum = conv_bias + jnp.zeros((seq_count, tok_count, rec_width), jnp.float32)
    for offset in range(CONV):
        conv_sum = (
            conv_sum
            + conv_kernel[offset]
            * ext_x[:, margin_len - offset : margin_len - offset + tok_count].astype(jnp.float32)
            * back_masks[offset]
        )
    conv_out = conv_sum.astype(jnp.bfloat16)
    conv_vals = conv_out.astype(jnp.float32)
    heads_in = conv_out.reshape(row_count, head_count, head_size)
    pre_rate = (
        jnp.einsum("rhi,hij->rhj", heads_in, rate_gate, preferred_element_type=jnp.float32).reshape(
            row_count, rec_width
        )
        + rate_bias
    )
    pre_input = (
        jnp.einsum(
            "rhi,hij->rhj", heads_in, input_gate, preferred_element_type=jnp.float32
        ).reshape(row_count, rec_width)
        + input_bias
    )
    (decays, in_scale), gate_back = jax.vjp(gate_values, pre_rate, pre_input, decay_param)
    in_scale3 = in_scale.reshape(seq_count, tok_count, rec_width)
    coeffs = decays.reshape(seq_count, tok_count, rec_width) * back_masks[1]
    inputs = in_scale3 * conv_vals
    cum_coef, local_state = lax.associative_scan(combine, (coeffs, inputs), axis=1)
    ones_row = jnp.ones((seq_count, rec_width), jnp.float32)
    zeros_row = jnp.zeros((seq_count, rec_width), jnp.float32)
    _, state_in = entering(
        (cum_coef[:, -1], local_state[:, -1]), "ctx", combine, (ones_row, zeros_row), False
    )
    states = local_state + cum_coef * state_in[:, None, :]
    state_rows = states.reshape(row_count, rec_width)
    mixed_in = (state_rows * y_act).astype(jnp.bfloat16)
    rec_part = matmul(mixed_in, w_out)
    col_start = lax.axis_index("tp") * part_width
    rec_total = lax.psum(rec_part, "tp")
    mid_rows = x_rows + rec_total
    normed_mid_f, norm_two_back = jax.vjp(rms_scale, mid_rows, gain_two.astype(jnp.float32))
    normed_mid = normed_mid_f.astype(jnp.bfloat16)
    gate_pre = matmul(normed_mid, w_gate)
    up_pre = matmul(normed_mid, w_up)
    gate_act, gate_act_back = jax.vjp(gelu_tanh, gate_pre)
    hidden = (gate_act * up_pre).astype(jnp.bfloat16)
    mlp_slice = lax.psum_scatter(matmul(hidden, w_down), "tp", scatter_dimension=1, tiled=True)
    mid_own = lax.dynamic_slice_in_dim(mid_rows, col_start, part_width, 1)
    block_out = (mid_own + mlp_slice).astype(jnp.bfloat16).reshape(seq_count, tok_count, part_width)
    cot_rows = out_cot.reshape(row_count, full_width)
    hid_grad = matmul_rt(cot_rows, w_down)
    grad_down = matmul_lt(hidden, cot_rows)
    gate_grad = gate_act_back(hid_grad * up_pre)[0].astype(jnp.bfloat16)
    up_grad = (hid_grad * gate_act).astype(jnp.bfloat16)
    grad_gate = matmul_lt(normed_mid, gate_grad)
    grad_up = matmul_lt(normed_mid, up_grad)
    mid_part = matmul_rt(gate_grad, w_gate) + matmul_rt(up_grad, w_up)
    mid_norm_grad = lax.psum(mid_part, "tp")
    mid_from_norm, gain_two_grad = norm_two_back(mid_norm_grad)
    mid_grad = cot_rows.astype(jnp.float32) + mid_from_norm
    rec_grad = mid_grad.astype(jnp.bfloat16)
    mixed_grad = matmul_rt(rec_grad, w_out)
    grad_out = matmul_lt(mixed_in, rec_grad)
    state_direct = (mixed_grad * y_act).reshape(seq_count, tok_count, rec_width)
    y_grad = y_back(mixed_grad * state_rows)[0].astype(jnp.bfloat16)
    grad_gelu = matmul_lt(normed, y_grad)
    in_part = matmul_rt(y_grad, w_gelu)
    next_coef = jnp.concatenate(
        [coeffs[:, 1:], jnp.ones((seq_count, 1, rec_width), jnp.float32)], axis=1
    )
    tail_coef, local_grad = lax.associative_scan(
        combine, (next_coef, state_direct), reverse=True, axis=1
    )
    head_coef = coeffs[:, 0]
    _, grad_in_state = entering(
        (head_coef * tail_coef[:, 0], head_coef * local_grad[:, 0]),
        "ctx",
        combine,
        (ones_row, zeros_row),
        True,
    )
    state_grad = local_grad + tail_coef * grad_in_state[:, None, :]
    prev_states = jnp.concatenate([state_in[:, None, :], states[:, :-1]], axis=1)
    decay_grad = (state_grad * prev_states * back_masks[1]).reshape(row_count, rec_width)
    scale_grad = (state_grad * conv_vals).reshape(row_count, rec_width)
    conv_direct = (state_grad * in_scale3).reshape(row_count, rec_width)
    rate_raw, input_raw, grad_decay = gate_back((decay_grad, scale_grad))
    rate_grad = rate_raw.astype(jnp.bfloat16)
    input_grad = input_raw.astype(jnp.bfloat16)
    rate_heads = rate_grad.reshape(row_count, head_count, head_size)
    input_heads = input_grad.reshape(row_count, head_count, head_size)
    grad_rate_gate = jnp.einsum(
        "rhi,rhj->hij", heads_in, rate_heads, preferred_element_type=jnp.float32
    )
    grad_input_gate = jnp.einsum(
        "rhi,rhj->hij", heads_in, input_heads, preferred_element_type=jnp.float32
    )
    grad_rate_bias = jnp.sum(rate_grad.astype(jnp.float32), axis=0)
    grad_input_bias = jnp.sum(input_grad.astype(jnp.float32), axis=0)
    gate_back_in = jnp.einsum(
        "rhj,hij->rhi", rate_heads, rate_gate, preferred_element_type=jnp.float32
    ) + jnp.einsum("rhj,hij->rhi", input_heads, input_gate, preferred_element_type=jnp.float32)
    conv_grad = (
        (conv_direct + gate_back_in.reshape(row_count, rec_width))
        .astype(jnp.bfloat16)
        .reshape(seq_count, tok_count, rec_width)
    )
    next_edge = from_behind(conv_grad[:, :margin_len, :], "ctx", -1)
    ext_grad = jnp.concatenate([conv_grad, next_edge], axis=1)
    conv_grad_f = conv_grad.astype(jnp.float32)
    branch_grad = jnp.zeros((seq_count, tok_count, rec_width), jnp.float32)
    kernel_rows = []
    for offset in range(CONV):
        branch_grad = (
            branch_grad
            + conv_kernel[offset]
            * ext_grad[:, offset : offset + tok_count].astype(jnp.float32)
            * ahead_masks[offset]
        )
        kernel_rows.append(
            jnp.sum(
                conv_grad_f
                * ext_x[:, margin_len - offset : margin_len - offset + tok_count].astype(
                    jnp.float32
                )
                * back_masks[offset],
                axis=(0, 1),
            )
        )
    grad_kernel = jnp.stack(kernel_rows)
    grad_conv = jnp.sum(conv_grad_f, axis=(0, 1))
    branch_low = branch_grad.astype(jnp.bfloat16).reshape(row_count, rec_width)
    grad_scan = matmul_lt(normed, branch_low)
    in_part = in_part + matmul_rt(branch_low, w_scan)
    in_from_norm, gain_one_part = norm_one_back(in_part)
    in_slice, gain_one_slice = (
        lax.psum_scatter(in_from_norm, "tp", scatter_dimension=1, tiled=True),
        lax.psum_scatter(gain_one_part, "tp", scatter_dimension=0, tiled=True),
    )
    grad_in = (lax.dynamic_slice_in_dim(mid_grad, col_start, part_width, 1) + in_slice).reshape(
        seq_count, tok_count, part_width
    )
    gain_two_slice = lax.dynamic_slice_in_dim(gain_two_grad, col_start, part_width, 0)
    grad_gelu_s, grad_scan_s, grad_out_s, grad_gate_s, grad_up_s, grad_down_s = (
        lax.psum_scatter(grad_gelu, ("fsdp", "ctx"), scatter_dimension=0, tiled=True),
        lax.psum_scatter(grad_scan, ("fsdp", "ctx"), scatter_dimension=0, tiled=True),
        lax.psum_scatter(grad_out, ("fsdp", "ctx"), scatter_dimension=1, tiled=True),
        lax.psum_scatter(grad_gate, ("fsdp", "ctx"), scatter_dimension=0, tiled=True),
        lax.psum_scatter(grad_up, ("fsdp", "ctx"), scatter_dimension=0, tiled=True),
        lax.psum_scatter(grad_down, ("fsdp", "ctx"), scatter_dimension=1, tiled=True),
    )
    (
        gain_one_total,
        gain_two_total,
        kernel_total,
        conv_total,
        rate_gate_total,
        input_gate_total,
        rate_bias_total,
        input_bias_total,
        decay_total,
    ) = lax.psum(
        (
            gain_one_slice,
            gain_two_slice,
            grad_kernel,
            grad_conv,
            grad_rate_gate,
            grad_input_gate,
            grad_rate_bias,
            grad_input_bias,
            grad_decay,
        ),
        ("fsdp", "ctx"),
    )
    return (
        block_out,
        grad_in,
        gain_one_total,
        gain_two_total,
        grad_gelu_s,
        grad_scan_s,
        grad_out_s,
        grad_gate_s,
        grad_up_s,
        grad_down_s,
        kernel_total,
        conv_total,
        rate_gate_total,
        input_gate_total,
        rate_bias_total,
        input_bias_total,
        decay_total,
    )


def solution(mesh):
    in_specs = (
        P("fsdp", "ctx", "tp"),
        P("fsdp", None),
        P("fsdp", "ctx", None),
        P("tp"),
        P("tp"),
        P(("fsdp", "ctx"), "tp"),
        P(("fsdp", "ctx"), "tp"),
        P("tp", ("fsdp", "ctx")),
        P(("fsdp", "ctx"), "tp"),
        P(("fsdp", "ctx"), "tp"),
        P("tp", ("fsdp", "ctx")),
        P(None, "tp"),
        P("tp"),
        P("tp", None, None),
        P("tp", None, None),
        P("tp"),
        P("tp"),
        P("tp"),
    )
    out_specs = (
        P("fsdp", "ctx", "tp"),
        P("fsdp", "ctx", "tp"),
        P("tp"),
        P("tp"),
        P(("fsdp", "ctx"), "tp"),
        P(("fsdp", "ctx"), "tp"),
        P("tp", ("fsdp", "ctx")),
        P(("fsdp", "ctx"), "tp"),
        P(("fsdp", "ctx"), "tp"),
        P("tp", ("fsdp", "ctx")),
        P(None, "tp"),
        P("tp"),
        P("tp", None, None),
        P("tp", None, None),
        P("tp"),
        P("tp"),
        P("tp"),
    )
    return jax.shard_map(shards, mesh=mesh, in_specs=in_specs, out_specs=out_specs, check_vma=False)
```

profile of v0, /device:TPU:0, one launch (start us, length us, event | category | flops | bytes accessed | tf_op | source)
XLA Modules:
  0.0 2524.0 jit_solution(14394685174451569282)
XLA Ops:
  10.7 13.5 all-gather.4
  26.8 66.3 %all-gather.14.cloned.1.call-done = bf16[4,256,2048]{2,1,0:T(8,128)(2,1)} async-done(((bf16[4,256,512]{2,1,0:T(8,128)(2,1)}), bf16[4,256,2048]{2,1,0:T(8,128)(2,1)}) %all-gather.14.cloned.1.call-update) | async-done | bytes 4194320 | tf_op jit(solution)/shard_map/all_gather | solution.py:93
  100.0 25.2 all-gather.16.cloned.1.call-done
  125.2 6.3 convolution_convert_fusion
  172.3 7.0 convert_multiply_fusion.8
  179.3 10.2 slice.580
  189.5 9.6 slice.581
  374.8 9.6 slice.635
  474.3 5.8 pad.212
  489.6 5.7 pad.229
  498.1 5.9 pad.228
  505.0 5.8 all-gather
  516.0 7.5 multiply_add_fusion.2
  527.0 9.7 multiply_convert_fusion.3
  536.7 9.1 fusion.116
  547.9 12.2 all-gather.5
  560.1 277.4 %all-reduce.73.cloned.1.call-done = f32[1024,2048]{1,0:T(8,128)} async-done(((f32[1024,2048]{1,0:T(8,128)}), f32[1024,2048]{1,0:T(8,128)}) %all-reduce.73.cloned.1.call-update) | async-done | bytes 8388624 | tf_op jit(solution)/shard_map/psum | solution.py:179
  837.5 5.9 multiply_reduce_fusion.2
  849.7 34.1 %all-gather.22.cloned.1.call-done = bf16[2048,1536]{1,0:T(8,128)(2,1)} async-done(((bf16[256,1536]{1,0:T(8,128)(2,1)}), bf16[2048,1536]{1,0:T(8,128)(2,1)}) %all-gather.22.cloned.1.call-update) | async-done | bytes 6291472 | tf_op jit(solution)/shard_map/all_gather | solution.py:101
  883.8 11.8 fusion.117
  895.7 35.6 %all-gather.24.cloned.1.call-done = bf16[2048,1536]{1,0:T(8,128)(2,1)} async-done(((bf16[256,1536]{1,0:T(8,128)(2,1)}), bf16[2048,1536]{1,0:T(8,128)(2,1)}) %all-gather.24.cloned.1.call-update) | async-done | bytes 6291472 | tf_op jit(solution)/shard_map/all_gather | solution.py:102
  931.3 11.9 fusion.118
  943.1 36.7 %all-gather.26.cloned.1.call-done = bf16[1536,2048]{1,0:T(8,128)(2,1)} async-done(((bf16[1536,256]{1,0:T(8,128)(2,1)}), bf16[1536,2048]{1,0:T(8,128)(2,1)}) %all-gather.26.cloned.1.call-update) | async-done | bytes 6291472 | tf_op jit(solution)/shard_map/all_gather | solution.py:103
  979.9 18.6 multiply_convert_fusion.1
  998.4 10.0 fusion.120
  1008.5 10.9 convolution_add_fusion.1
  1023.8 9.7 slice.657
  1033.4 9.6 slice.664
  1043.0 9.5 slice.655
  1053.1 12.8 slice.658
  1065.9 12.7 slice.665
  1078.7 12.8 slice.656
  1091.5 11.9 fusion.119
  1103.5 206.9 %all-reduce.75.cloned.1.call-done = f32[1024,2048]{1,0:T(8,128)} async-done(((f32[1024,2048]{1,0:T(8,128)}), f32[1024,2048]{1,0:T(8,128)}) %all-reduce.75.cloned.1.call-update) | async-done | bytes 8388624 | tf_op jit(solution)/shard_map/psum | solution.py:198
  1310.4 7.7 multiply_reduce_fusion
  1325.5 11.8 fusion.72
  1340.8 9.5 slice.659
  1350.4 9.6 slice.661
  1359.9 12.8 slice.660
  1372.7 12.8 slice.662
  1480.8 9.5 slice.717
  1641.5 12.8 slice.718
  1669.5 5.7 pad.260
  1695.7 24.7 rev.15
  1720.5 24.8 rev.14
  1747.6 11.8 multiply_reduce_fusion.3
  1778.6 7.5 fusion.60
  1799.5 10.8 fusion.43
  1831.7 9.1 fusion.62
  1842.2 7.3 fusion.128
  1850.9 8.0 fusion.22
  1859.0 12.5 fusion.122
  1871.8 12.6 fusion.123
  1884.4 12.2 fusion.124
  1899.4 9.0 all-reduce.66
  1908.5 26.4 %all-reduce.67 = (f32[512]{0:T(512)}, f32[512]{0:T(512)}, f32[4,704]{1,0:T(4,128)}, f32[704]{0:T(1024)}, f32[704]{0:T(1024)}, /*index=5*/f32[704]{0:T(1024)}, f32[704]{0:T(1024)}) all-reduce(f32[512]{0:T(512)S(1)} %dynamic-slice.3, f32[512]{0:T(512)S(1)} %dynamic_slice.43, ...), channel_id=1, replica_groups=mesh['fsdp'=2,'ctx'=4,'tp'=4] {'fsdp','ctx'}, use_global_device_ids=true, to_apply=%region_14.15 | all-reduce | flops 6656 | bytes 53248 | tf_op jit(solution)/shard_map/psum | solution.py:302
  1938.5 33.6 %reduce-scatter.11.cloned.1.call-done = f32[1024,512]{1,0:T(8,128)} async-done(((f32[1024,2048]{1,0:T(8,128)}), f32[1024,512]{1,0:T(8,128)}) %reduce-scatter.11.cloned.1.call-update) | async-done | bytes 2097168 | tf_op jit(solution)/shard_map/reduce_scatter | solution.py:277
  1976.2 58.8 %all-reduce.77.cloned.1.call-done = (f32[4,176,176]{2,1,0:T(8,128)}, f32[4,176,176]{2,1,0:T(8,128)}) async-done(((f32[4,176,176]{2,1,0:T(8,128)}, f32[4,176,176]{2,1,0:T(8,128)}), (f32[4,176,176]{2,1,0:T(8,128)}, f32[4,176,176]{2,1,0:T(8,128)})) %all-reduce.77.cloned.1.call-update) | async-done | bytes 991248 | tf_op jit(solution)/shard_map/psum | solution.py:302
  2034.9 62.7 %reduce-scatter.17.cloned.1.call-done = f32[704,256]{1,0:T(8,128)} async-done(((f32[704,2048]{1,0:T(8,128)}), f32[704,256]{1,0:T(8,128)}) %reduce-scatter.17.cloned.1.call-update) | async-done | bytes 720912 | tf_op jit(solution)/shard_map/reduce_scatter | solution.py:287
  2097.6 63.0 %reduce-scatter.13.cloned.1.call-done = f32[256,704]{0,1:T(8,128)} async-done(((f32[2048,704]{0,1:T(8,128)}), f32[256,704]{0,1:T(8,128)}) %reduce-scatter.13.cloned.1.call-update) | async-done | bytes 720912 | tf_op jit(solution)/shard_map/reduce_scatter | solution.py:285
  2160.6 63.3 %reduce-scatter.15.cloned.1.call-done = f32[256,704]{0,1:T(8,128)} async-done(((f32[2048,704]{0,1:T(8,128)}), f32[256,704]{0,1:T(8,128)}) %reduce-scatter.15.cloned.1.call-update) | async-done | bytes 720912 | tf_op jit(solution)/shard_map/reduce_scatter | solution.py:286
  2223.9 96.3 %reduce-scatter.19.cloned.1.call-done = f32[256,1536]{1,0:T(8,128)} async-done(((f32[2048,1536]{1,0:T(8,128)}), f32[256,1536]{1,0:T(8,128)}) %reduce-scatter.19.cloned.1.call-update) | async-done | bytes 1572880 | tf_op jit(solution)/shard_map/reduce_scatter | solution.py:288
  2320.2 96.3 %reduce-scatter.21.cloned.1.call-done = f32[256,1536]{1,0:T(8,128)} async-done(((f32[2048,1536]{1,0:T(8,128)}), f32[256,1536]{1,0:T(8,128)}) %reduce-scatter.21.cloned.1.call-update) | async-done | bytes 1572880 | tf_op jit(solution)/shard_map/reduce_scatter | solution.py:289
  2416.5 96.4 %reduce-scatter.23.cloned.1.call-done = f32[1536,256]{1,0:T(8,128)} async-done(((f32[1536,2048]{1,0:T(8,128)}), f32[1536,256]{1,0:T(8,128)}) %reduce-scatter.23.cloned.1.call-update) | async-done | bytes 1572880 | tf_op jit(solution)/shard_map/reduce_scatter | solution.py:290
  (599 shorter events, 724.4 us)
Async XLA Ops:
  7.2 141.0 %copy-start = (bf16[4,176,176]{2,1,0:T(8,128)(2,1)S(1)}, bf16[4,176,176]{2,1,0:T(8,128)(2,1)}, u32[]{:S(2)}) copy-start(bf16[4,176,176]{2,1,0:T(8,128)(2,1)} %param.35) | copy-start | bytes 743428
  7.2 85.9 %all-gather.14.cloned.1.call-start = ((), (), s32[]{:S(2)}) async-start(), calls=%async_computation.8 | async-start | bytes 5242880 | tf_op jit(solution)/shard_map/all_gather | solution.py:93
  7.9 117.3 %all-gather.16.cloned.1.call-start = ((), (), s32[]{:S(2)}) async-start(), calls=%async_computation.9 | async-start | bytes 3244032 | tf_op jit(solution)/shard_map/all_gather | solution.py:99
  8.7 518.3 %all-gather.18.cloned.1.call-start = ((), (), s32[]{:S(2)}) async-start(), calls=%async_computation.10 | async-start | bytes 3244032 | tf_op jit(solution)/shard_map/all_gather | solution.py:98
  9.4 527.2 %all-gather.20.cloned.1.call-start = ((), (), s32[]{:S(2)}) async-start(), calls=%async_computation.11 | async-start | bytes 3244032 | tf_op jit(solution)/shard_map/all_gather | solution.py:100
  10.0 827.5 %all-reduce.73.cloned.1.call-start = ((), (), s32[]{:S(2)}) async-start(), calls=%async_computation.12 | async-start | bytes 16777216 | tf_op jit(solution)/shard_map/psum | solution.py:179
  24.3 75.8 %copy-start.51 = (f32[4,1,512]{2,1,0:T(1,128)}, f32[4,1,512]{2,1,0:T(1,128)S(1)}, u32[]{:S(2)}) copy-start(f32[4,1,512]{2,1,0:T(1,128)S(1)} %convert_element_type.180) | copy-start | bytes 24580
  25.2 113.3 %copy-start.71 = (f32[704]{0:T(1024)}, f32[704]{0:T(1024)S(1)}, u32[]{:S(2)}) copy-start(f32[704]{0:T(1024)S(1)} %get-tuple-element.255) | copy-start | bytes 8452
  25.2 113.3 %copy-start.73 = (f32[704]{0:T(1024)}, f32[704]{0:T(1024)S(1)}, u32[]{:S(2)}) copy-start(f32[704]{0:T(1024)S(1)} %get-tuple-element.256) | copy-start | bytes 8452
  25.2 113.3 %copy-start.75 = (f32[704]{0:T(1024)}, f32[704]{0:T(1024)S(1)}, u32[]{:S(2)}) copy-start(f32[704]{0:T(1024)S(1)} %get-tuple-element.257) | copy-start | bytes 8452
  25.2 113.3 %copy-start.77 = (f32[704]{0:T(1024)}, f32[704]{0:T(1024)S(1)}, u32[]{:S(2)}) copy-start(f32[704]{0:T(1024)S(1)} %get-tuple-element.258) | copy-start | bytes 8452
  25.9 993.5 %copy-start.49 = (f32[704]{0:T(1024)}, f32[704]{0:T(1024)S(1)}, u32[]{:S(2)}) copy-start(f32[704]{0:T(1024)S(1)} %fusion.94) | copy-start | bytes 8452
  132.6 6.9 copy-start.102
  134.1 4.3 collective-permute-start
  137.2 8.0 copy-start.79
  137.2 8.0 copy-start.81
  137.2 35.1 %copy-start.47 = (f32[4,256]{1,0:T(4,128)}, f32[4,256]{1,0:T(4,128)S(1)}, u32[]{:S(2)}) copy-start(f32[4,256]{1,0:T(4,128)S(1)} %get-tuple-element.377) | copy-start | bytes 12292
  138.4 9.7 copy-start.11
  158.1 14.2 copy-start.4
  179.3 19.8 copy-start.6
  301.5 37.3 %copy-start.67 = (f32[4,1,704]{2,1,0:T(1,128)S(1)}, f32[4,1,704]{2,1,0:T(1,128)}, u32[]{:S(2)}) copy-start(f32[4,1,704]{2,1,0:T(1,128)} %slice.752) | copy-start | bytes 33796
  403.2 6.3 copy-start.70
  545.8 338.1 %all-gather.22.cloned.1.call-start = ((), (), s32[]{:S(2)}) async-start(), calls=%async_computation.13 | async-start | bytes 7077888 | tf_op jit(solution)/shard_map/all_gather | solution.py:101
  546.4 384.9 %all-gather.24.cloned.1.call-start = ((), (), s32[]{:S(2)}) async-start(), calls=%async_computation.14 | async-start | bytes 7077888 | tf_op jit(solution)/shard_map/all_gather | solution.py:102
  547.1 432.8 %all-gather.26.cloned.1.call-start = ((), (), s32[]{:S(2)}) async-start(), calls=%async_computation.15 | async-start | bytes 7077888 | tf_op jit(solution)/shard_map/all_gather | solution.py:103
  547.9 762.5 %all-reduce.75.cloned.1.call-start = ((), (), s32[]{:S(2)}) async-start(), calls=%async_computation.17 | async-start | bytes 16777216 | tf_op jit(solution)/shard_map/psum | solution.py:198
  560.1 750.3 %copy-start.42 = (f32[4,1,512]{2,1,0:T(1,128)}, f32[4,1,512]{2,1,0:T(1,128)S(1)}, u32[]{:S(2)}) copy-start(f32[4,1,512]{2,1,0:T(1,128)S(1)} %convert_element_type.181) | copy-start | bytes 24580
  843.4 467.0 %copy-start.53 = (f32[1024]{0:T(1024)}, f32[1024]{0:T(1024)S(1)}, u32[]{:S(2)}) copy-start(f32[1024]{0:T(1024)S(1)} %fusion.101) | copy-start | bytes 12292
  998.4 10.0 copy-start.112
  998.4 10.0 copy-start.105
  1019.4 915.5 %reduce-scatter.9.cloned.1.call-start = ((), (), s32[]{:S(2)}) async-start(), calls=%async_computation.16 | async-start | bytes 10485760 | tf_op jit(solution)/shard_map/reduce_scatter | solution.py:187
  1103.4 868.7 %reduce-scatter.11.cloned.1.call-start = ((), (), s32[]{:S(2)}) async-start(), calls=%async_computation.18 | async-start | bytes 10485760 | tf_op jit(solution)/shard_map/reduce_scatter | solution.py:277
  1310.4 9.0 copy-start.9
  1310.4 10.2 copy-start.30
  1325.5 11.8 copy-start.15
  1523.2 30.4 %copy-start.66 = (f32[4,1,704]{2,1,0:T(1,128)S(1)}, f32[4,1,704]{2,1,0:T(1,128)}, u32[]{:S(2)}) copy-start(f32[4,1,704]{2,1,0:T(1,128)} %slice.804) | copy-start | bytes 33796
  1531.5 30.1 %copy-start.65 = (f32[4,1,704]{2,1,0:T(1,128)S(1)}, f32[4,1,704]{2,1,0:T(1,128)}, u32[]{:S(2)}) copy-start(f32[4,1,704]{2,1,0:T(1,128)} %slice.829) | copy-start | bytes 33796
  1566.9 10.0 copy-start.69
  1574.4 15.6 copy-start.68
  1615.5 5.7 copy-start.62
  1654.3 5.5 copy-start.61
  1675.2 5.1 copy-start.20
  1675.2 5.4 copy-start.21
  1720.4 24.9 copy-start.39
  1720.4 27.1 %copy-start.5 = (f32[4,256,704]{2,1,0:T(8,128)S(1)}, f32[4,256,704]{2,1,0:T(8,128)}, u32[]{:S(2)}) copy-start(f32[4,256,704]{2,1,0:T(8,128)} %copy-done.4) | copy-start | bytes 8650756
  1720.4 27.1 %copy-start.48 = (f32[4,256]{1,0:T(4,128)S(1)}, f32[4,256]{1,0:T(4,128)}, u32[]{:S(2)}) copy-start(f32[4,256]{1,0:T(4,128)} %copy-done.47) | copy-start | bytes 12292
  1720.4 27.2 %copy-start.50 = (f32[704]{0:T(1024)S(1)}, f32[704]{0:T(1024)}, u32[]{:S(2)}) copy-start(f32[704]{0:T(1024)} %copy-done.49) | copy-start | bytes 8452
  1720.4 27.2 %copy-start.56 = (f32[704]{0:T(1024)S(1)}, f32[704]{0:T(1024)}, u32[]{:S(2)}) copy-start(f32[704]{0:T(1024)} %param.38) | copy-start | bytes 8452
  1720.5 27.2 %copy-start.59 = (f32[704]{0:T(1024)S(1)}, f32[704]{0:T(1024)}, u32[]{:S(2)}) copy-start(f32[704]{0:T(1024)} %param.37) | copy-start | bytes 8452
  1720.5 27.2 %copy-start.60 = (f32[4,1,704]{2,1,0:T(1,128)S(1)}, f32[4,1,704]{2,1,0:T(1,128)}, u32[]{:S(2)}) copy-start(f32[4,1,704]{2,1,0:T(1,128)} %broadcast_in_dim.10) | copy-start | bytes 33796
  1799.4 12.1 copy-start.107
  1799.5 12.1 copy-start.110
  1810.3 5.0 collective-permute-start.1
  1811.7 6.1 copy-start.3
  1826.9 208.0 %all-reduce.77.cloned.1.call-start = ((), (), s32[]{:S(2)}) async-start(), calls=%async_computation.25 | async-start | bytes 2883584 | tf_op jit(solution)/shard_map/psum | solution.py:302
  1831.7 265.9 %reduce-scatter.17.cloned.1.call-start = ((), (), s32[]{:S(2)}) async-start(), calls=%async_computation.21 | async-start | bytes 6488064 | tf_op jit(solution)/shard_map/reduce_scatter | solution.py:287
  1840.8 319.8 %reduce-scatter.13.cloned.1.call-start = ((), (), s32[]{:S(2)}) async-start(), calls=%async_computation.19 | async-start | bytes 6488064 | tf_op jit(solution)/shard_map/reduce_scatter | solution.py:285
  1849.5 374.4 %reduce-scatter.15.cloned.1.call-start = ((), (), s32[]{:S(2)}) async-start(), calls=%async_computation.20 | async-start | bytes 6488064 | tf_op jit(solution)/shard_map/reduce_scatter | solution.py:286
  1858.9 461.3 %reduce-scatter.19.cloned.1.call-start = ((), (), s32[]{:S(2)}) async-start(), calls=%async_computation.22 | async-start | bytes 14155776 | tf_op jit(solution)/shard_map/reduce_scatter | solution.py:288
  1871.5 545.0 %reduce-scatter.21.cloned.1.call-start = ((), (), s32[]{:S(2)}) async-start(), calls=%async_computation.23 | async-start | bytes 14155776 | tf_op jit(solution)/shard_map/reduce_scatter | solution.py:289
  1884.3 628.6 %reduce-scatter.23.cloned.1.call-start = ((), (), s32[]{:S(2)}) async-start(), calls=%async_computation.24 | async-start | bytes 14155776 | tf_op jit(solution)/shard_map/reduce_scatter | solution.py:290
  1896.7 11.8 copy-start.95
  1896.7 11.8 copy-start.96
  1896.7 11.8 copy-start.97
  (69 other events, 214.7 us)
Sparse Core Ops, SparseCore 0:
  9.6 83.4 all-gather.13
  95.0 30.1 all-gather.15
  127.1 31.8 all-gather.17
  160.7 31.6 all-gather.19
  545.9 291.5 all-reduce.72
  839.3 44.5 all-gather.21
  885.7 45.5 all-gather.23
  933.2 46.6 all-gather.25
  1019.5 290.8 all-reduce.74
  1312.6 143.4 reduce-scatter.8
  1827.0 145.0 reduce-scatter.10
  1975.8 59.0 all-reduce.76
  2039.3 58.2 reduce-scatter.16
  2101.5 59.0 reduce-scatter.12
  2164.8 58.9 reduce-scatter.14
  2227.8 92.3 reduce-scatter.18
  2324.1 92.3 reduce-scatter.20
  2420.5 92.3 reduce-scatter.22
where the time goes:
time: 2550 us; the launch traced here: 2520 us
  waiting for transfers between devices  1260 us (49%)
  local copies, waits for them, and re-layouts  706 us (28%)
  other arithmetic  262 us (10%)
  matrix products  194 us (8%)
  blocking collectives  83 us (3%)
    psum x1, waiting for transfers between devices, shards(): rec_total = lax.psum(rec_part, 'tp')  277 us
    slice x57, local copies, waits for them, and re-layouts, shards(): lax.associative_scan(combine, (next_coef, state_direct), reverse=True, ax...  215 us
    psum x1, waiting for transfers between devices, shards(): mid_norm_grad = lax.psum(mid_part, 'tp')  207 us
    slice x52, local copies, waits for them, and re-layouts, shards(): lax.associative_scan(combine, (coeffs, inputs), axis=1)  128 us
    pad x28, local copies, waits for them, and re-layouts, shards(): lax.associative_scan(combine, (coeffs, inputs), axis=1)  110 us
    pad x28, local copies, waits for them, and re-layouts, shards(): lax.associative_scan(combine, (next_coef, state_direct), reverse=True, ax...  108 us
    reduce_scatter x1, waiting for transfers between devices, shards(): lax.psum_scatter(grad_down, ('fsdp', 'ctx'), scatter_dimension=1, tiled=T...  96.4 us
    reduce_scatter x1, waiting for transfers between devices, shards(): lax.psum_scatter(grad_up, ('fsdp', 'ctx'), scatter_dimension=0, tiled=True)  96.3 us
  transfers between devices with their start and end apart: 20, of which 15 were waited for; matrix products, arithmetic and copies ran while one was open for 43% of the time, Pallas kernels for 0%

commit v1 on v0

--- a/solution.py
+++ b/solution.py
@@ -300,18 +300,21 @@
         input_bias_total,
         decay_total,
     ) = lax.psum(
-        (
-            gain_one_slice,
-            gain_two_slice,
-            grad_kernel,
-            grad_conv,
-            grad_rate_gate,
-            grad_input_gate,
-            grad_rate_bias,
-            grad_input_bias,
-            grad_decay,
+        lax.psum(
+            (
+                gain_one_slice,
+                gain_two_slice,
+                grad_kernel,
+                grad_conv,
+                grad_rate_gate,
+                grad_input_gate,
+                grad_rate_bias,
+                grad_input_bias,
+                grad_decay,
+            ),
+            "ctx",
         ),
-        ("fsdp", "ctx"),
+        "fsdp",
     )
     return (
         block_out,

time: 2550 us -> 2690 us (1.055)
  waiting for transfers between devices: 1260 us -> 1410 us
    reduce_scatter x1, waiting for transfers between devices: 33.6 us -> 144 us  [shards(): lax.psum_scatter(in_from_norm, 'tp', scatter_dimension=1, tiled=True)]
    psum x1, waiting for transfers between devices: 58.8 us -> 0.02 us  [shards(): lax.psum((gain_one_slice, gain_two_slice, grad_kernel, grad_conv, grad_ra...]
    psum x0 -> x1, waiting for transfers between devices: none -> 47.9 us  [shards(): lax.psum(lax.psum((gain_one_slice, gain_two_slice, grad_kernel, grad_conv...]
    reduce_scatter x1, waiting for transfers between devices: 0.01 us -> 36.6 us  [shards(): lax.psum_scatter(matmul(hidden, w_down), 'tp', scatter_dimension=1, tiled...]
  transfers between devices with their start and end apart: 20 -> 21, of which waited for: 15 -> 16; matrix products, arithmetic and copies ran while one was open for 43% -> 24% of each run, Pallas kernels for 0% -> 0%
where the time goes in v1:
time: 2690 us; the launch traced here: 2660 us
  waiting for transfers between devices  1410 us (52%)
  local copies, waits for them, and re-layouts  698 us (26%)
  other arithmetic  263 us (10%)
  matrix products  194 us (7%)
  blocking collectives  79.1 us (3%)
    psum x1, waiting for transfers between devices, shards(): rec_total = lax.psum(rec_part, 'tp')  277 us
    psum x1, waiting for transfers between devices, shards(): mid_norm_grad = lax.psum(mid_part, 'tp')  219 us
    slice x57, local copies, waits for them, and re-layouts, shards(): lax.associative_scan(combine, (next_coef, state_direct), reverse=True, ax...  216 us
    reduce_scatter x1, waiting for transfers between devices, shards(): lax.psum_scatter(in_from_norm, 'tp', scatter_dimension=1, tiled=True)  144 us
    slice x52, local copies, waits for them, and re-layouts, shards(): lax.associative_scan(combine, (coeffs, inputs), axis=1)  127 us
    pad x28, local copies, waits for them, and re-layouts, shards(): lax.associative_scan(combine, (coeffs, inputs), axis=1)  109 us
    pad x28, local copies, waits for them, and re-layouts, shards(): lax.associative_scan(combine, (next_coef, state_direct), reverse=True, ax...  108 us
    reduce_scatter x1, waiting for transfers between devices, shards(): lax.psum_scatter(grad_down, ('fsdp', 'ctx'), scatter_dimension=1, tiled=T...  96.5 us
  transfers between devices with their start and end apart: 21, of which 16 were waited for; matrix products, arithmetic and copies ran while one was open for 24% of the time, Pallas kernels for 0%

profile of v1, /device:TPU:0, one launch (start us, length us, event | category | flops | bytes accessed | tf_op | source)
XLA Modules:
  0.0 2662.7 jit_solution(16247939536372966473)
XLA Ops:
  10.7 13.5 all-gather.4
  26.8 66.3 %all-gather.14.cloned.1.call-done = bf16[4,256,2048]{2,1,0:T(8,128)(2,1)} async-done(((bf16[4,256,512]{2,1,0:T(8,128)(2,1)}), bf16[4,256,2048]{2,1,0:T(8,128)(2,1)}) %all-gather.14.cloned.1.call-update) | async-done | bytes 4194320 | tf_op jit(solution)/shard_map/all_gather | solution.py:93
  100.0 25.2 all-gather.16.cloned.1.call-done
  125.2 6.3 convolution_convert_fusion
  172.8 7.1 convert_multiply_fusion.8
  179.9 9.9 slice.580
  189.8 9.6 slice.581
  374.6 9.6 slice.635
  489.5 5.7 pad.229
  515.5 7.2 multiply_add_fusion.2
  526.2 9.7 multiply_convert_fusion.3
  535.8 9.1 fusion.116
  547.1 12.2 all-gather.5
  559.4 277.2 %all-reduce.76.cloned.1.call-done = f32[1024,2048]{1,0:T(8,128)} async-done(((f32[1024,2048]{1,0:T(8,128)}), f32[1024,2048]{1,0:T(8,128)}) %all-reduce.76.cloned.1.call-update) | async-done | bytes 8388624 | tf_op jit(solution)/shard_map/psum | solution.py:179
  836.5 5.7 multiply_reduce_fusion.2
  848.6 34.2 %all-gather.22.cloned.1.call-done = bf16[2048,1536]{1,0:T(8,128)(2,1)} async-done(((bf16[256,1536]{1,0:T(8,128)(2,1)}), bf16[2048,1536]{1,0:T(8,128)(2,1)}) %all-gather.22.cloned.1.call-update) | async-done | bytes 6291472 | tf_op jit(solution)/shard_map/all_gather | solution.py:101
  882.8 12.1 fusion.117
  895.0 35.3 %all-gather.24.cloned.1.call-done = bf16[2048,1536]{1,0:T(8,128)(2,1)} async-done(((bf16[256,1536]{1,0:T(8,128)(2,1)}), bf16[2048,1536]{1,0:T(8,128)(2,1)}) %all-gather.24.cloned.1.call-update) | async-done | bytes 6291472 | tf_op jit(solution)/shard_map/all_gather | solution.py:102
  930.3 11.7 fusion.118
  942.0 36.9 %all-gather.26.cloned.1.call-done = bf16[1536,2048]{1,0:T(8,128)(2,1)} async-done(((bf16[1536,256]{1,0:T(8,128)(2,1)}), bf16[1536,2048]{1,0:T(8,128)(2,1)}) %all-gather.26.cloned.1.call-update) | async-done | bytes 6291472 | tf_op jit(solution)/shard_map/all_gather | solution.py:103
  978.9 18.5 multiply_convert_fusion.1
  997.4 10.0 fusion.120
  1007.4 10.5 convolution_add_fusion.1
  1022.2 9.8 slice.657
  1032.1 9.6 slice.664
  1041.6 9.5 slice.655
  1051.8 12.9 slice.658
  1064.7 12.7 slice.665
  1077.4 12.8 slice.656
  1090.2 218.7 %all-reduce.78.cloned.1.call-done = f32[1024,2048]{1,0:T(8,128)} async-done(((f32[1024,2048]{1,0:T(8,128)}), f32[1024,2048]{1,0:T(8,128)}) %all-reduce.78.cloned.1.call-update) | async-done | bytes 8388624 | tf_op jit(solution)/shard_map/psum | solution.py:198
  1309.0 7.7 multiply_reduce_fusion
  1323.3 11.8 fusion.72
  1338.6 9.6 slice.659
  1348.1 9.5 slice.661
  1357.7 12.8 slice.660
  1370.5 12.8 slice.662
  1482.1 9.5 slice.717
  1632.3 5.8 pad.245
  1638.1 12.9 slice.718
  1657.8 5.7 pad.244
  1702.8 15.6 rev.15
  1718.4 25.0 rev.14
  1743.4 11.9 multiply_reduce_fusion.3
  1774.3 7.6 fusion.60
  1785.9 11.7 fusion.119
  1811.5 10.6 fusion.43
  1840.0 8.2 fusion.62
  1849.6 7.1 fusion.128
  1857.4 8.1 fusion.22
  1865.6 12.6 fusion.122
  1878.3 12.5 fusion.123
  1891.1 12.3 fusion.124
  1906.2 10.3 all-reduce.66
  1916.6 11.3 all-reduce.67
  1927.9 9.1 all-reduce.69
  1937.0 36.6 %reduce-scatter.9.cloned.1.call-done = f32[1024,512]{1,0:T(8,128)} async-done(((f32[1024,2048]{1,0:T(8,128)}), f32[1024,512]{1,0:T(8,128)}) %reduce-scatter.9.cloned.1.call-update) | async-done | bytes 2097168 | tf_op jit(solution)/shard_map/reduce_scatter | solution.py:187
  1977.1 143.9 %reduce-scatter.11.cloned.1.call-done = f32[1024,512]{1,0:T(8,128)} async-done(((f32[1024,2048]{1,0:T(8,128)}), f32[1024,512]{1,0:T(8,128)}) %reduce-scatter.11.cloned.1.call-update) | async-done | bytes 2097168 | tf_op jit(solution)/shard_map/reduce_scatter | solution.py:277
  2125.0 47.9 %all-reduce.82.cloned.1.call-done = (f32[4,176,176]{2,1,0:T(8,128)}, f32[4,176,176]{2,1,0:T(8,128)}) async-done(((f32[4,176,176]{2,1,0:T(8,128)}, f32[4,176,176]{2,1,0:T(8,128)}), (f32[4,176,176]{2,1,0:T(8,128)}, f32[4,176,176]{2,1,0:T(8,128)})) %all-reduce.82.cloned.1.call-update) | async-done | bytes 991248 | tf_op jit(solution)/shard_map/psum | solution.py:302
  2172.9 63.4 %reduce-scatter.17.cloned.1.call-done = f32[704,256]{1,0:T(8,128)} async-done(((f32[704,2048]{1,0:T(8,128)}), f32[704,256]{1,0:T(8,128)}) %reduce-scatter.17.cloned.1.call-update) | async-done | bytes 720912 | tf_op jit(solution)/shard_map/reduce_scatter | solution.py:287
  2236.2 62.9 %reduce-scatter.13.cloned.1.call-done = f32[256,704]{0,1:T(8,128)} async-done(((f32[2048,704]{0,1:T(8,128)}), f32[256,704]{0,1:T(8,128)}) %reduce-scatter.13.cloned.1.call-update) | async-done | bytes 720912 | tf_op jit(solution)/shard_map/reduce_scatter | solution.py:285
  2299.1 63.3 %reduce-scatter.15.cloned.1.call-done = f32[256,704]{0,1:T(8,128)} async-done(((f32[2048,704]{0,1:T(8,128)}), f32[256,704]{0,1:T(8,128)}) %reduce-scatter.15.cloned.1.call-update) | async-done | bytes 720912 | tf_op jit(solution)/shard_map/reduce_scatter | solution.py:286
  2362.5 96.3 %reduce-scatter.19.cloned.1.call-done = f32[256,1536]{1,0:T(8,128)} async-done(((f32[2048,1536]{1,0:T(8,128)}), f32[256,1536]{1,0:T(8,128)}) %reduce-scatter.19.cloned.1.call-update) | async-done | bytes 1572880 | tf_op jit(solution)/shard_map/reduce_scatter | solution.py:288
  2458.8 96.4 %reduce-scatter.21.cloned.1.call-done = f32[256,1536]{1,0:T(8,128)} async-done(((f32[2048,1536]{1,0:T(8,128)}), f32[256,1536]{1,0:T(8,128)}) %reduce-scatter.21.cloned.1.call-update) | async-done | bytes 1572880 | tf_op jit(solution)/shard_map/reduce_scatter | solution.py:289
  2555.2 96.5 %reduce-scatter.23.cloned.1.call-done = f32[1536,256]{1,0:T(8,128)} async-done(((f32[1536,2048]{1,0:T(8,128)}), f32[1536,256]{1,0:T(8,128)}) %reduce-scatter.23.cloned.1.call-update) | async-done | bytes 1572880 | tf_op jit(solution)/shard_map/reduce_scatter | solution.py:290
  (595 shorter events, 741.8 us)
Async XLA Ops:
  7.2 141.4 %copy-start = (bf16[4,176,176]{2,1,0:T(8,128)(2,1)S(1)}, bf16[4,176,176]{2,1,0:T(8,128)(2,1)}, u32[]{:S(2)}) copy-start(bf16[4,176,176]{2,1,0:T(8,128)(2,1)} %param.35) | copy-start | bytes 743428
  7.2 85.9 %all-gather.14.cloned.1.call-start = ((), (), s32[]{:S(2)}) async-start(), calls=%async_computation.8 | async-start | bytes 5242880 | tf_op jit(solution)/shard_map/all_gather | solution.py:93
  7.9 117.3 %all-gather.16.cloned.1.call-start = ((), (), s32[]{:S(2)}) async-start(), calls=%async_computation.9 | async-start | bytes 3244032 | tf_op jit(solution)/shard_map/all_gather | solution.py:99
  8.7 517.5 %all-gather.18.cloned.1.call-start = ((), (), s32[]{:S(2)}) async-start(), calls=%async_computation.10 | async-start | bytes 3244032 | tf_op jit(solution)/shard_map/all_gather | solution.py:98
  9.4 526.4 %all-gather.20.cloned.1.call-start = ((), (), s32[]{:S(2)}) async-start(), calls=%async_computation.11 | async-start | bytes 3244032 | tf_op jit(solution)/shard_map/all_gather | solution.py:100
  10.0 826.5 %all-reduce.76.cloned.1.call-start = ((), (), s32[]{:S(2)}) async-start(), calls=%async_computation.12 | async-start | bytes 16777216 | tf_op jit(solution)/shard_map/psum | solution.py:179
  24.3 75.7 %copy-start.45 = (f32[4,1,512]{2,1,0:T(1,128)}, f32[4,1,512]{2,1,0:T(1,128)S(1)}, u32[]{:S(2)}) copy-start(f32[4,1,512]{2,1,0:T(1,128)S(1)} %convert_element_type.180) | copy-start | bytes 24580
  25.2 113.6 %copy-start.67 = (f32[704]{0:T(1024)}, f32[704]{0:T(1024)S(1)}, u32[]{:S(2)}) copy-start(f32[704]{0:T(1024)S(1)} %get-tuple-element.255) | copy-start | bytes 8452
  25.2 113.6 %copy-start.69 = (f32[704]{0:T(1024)}, f32[704]{0:T(1024)S(1)}, u32[]{:S(2)}) copy-start(f32[704]{0:T(1024)S(1)} %get-tuple-element.256) | copy-start | bytes 8452
  25.2 113.6 %copy-start.71 = (f32[704]{0:T(1024)}, f32[704]{0:T(1024)S(1)}, u32[]{:S(2)}) copy-start(f32[704]{0:T(1024)S(1)} %get-tuple-element.257) | copy-start | bytes 8452
  25.2 113.6 %copy-start.73 = (f32[704]{0:T(1024)}, f32[704]{0:T(1024)S(1)}, u32[]{:S(2)}) copy-start(f32[704]{0:T(1024)S(1)} %get-tuple-element.258) | copy-start | bytes 8452
  25.9 992.1 %copy-start.43 = (f32[704]{0:T(1024)}, f32[704]{0:T(1024)S(1)}, u32[]{:S(2)}) copy-start(f32[704]{0:T(1024)S(1)} %fusion.94) | copy-start | bytes 8452
  132.6 7.4 copy-start.98
  134.2 4.6 collective-permute-start
  137.5 8.1 copy-start.75
  137.5 8.1 copy-start.77
  137.5 35.3 %copy-start.41 = (f32[4,256]{1,0:T(4,128)}, f32[4,256]{1,0:T(4,128)S(1)}, u32[]{:S(2)}) copy-start(f32[4,256]{1,0:T(4,128)S(1)} %get-tuple-element.386) | copy-start | bytes 12292
  138.8 9.8 copy-start.11
  158.7 14.1 copy-start.4
  179.9 19.5 copy-start.6
  301.7 37.1 %copy-start.61 = (f32[4,1,704]{2,1,0:T(1,128)S(1)}, f32[4,1,704]{2,1,0:T(1,128)}, u32[]{:S(2)}) copy-start(f32[4,1,704]{2,1,0:T(1,128)} %slice.752) | copy-start | bytes 33796
  403.0 6.3 copy-start.66
  544.9 337.9 %all-gather.22.cloned.1.call-start = ((), (), s32[]{:S(2)}) async-start(), calls=%async_computation.13 | async-start | bytes 7077888 | tf_op jit(solution)/shard_map/all_gather | solution.py:101
  545.5 384.8 %all-gather.24.cloned.1.call-start = ((), (), s32[]{:S(2)}) async-start(), calls=%async_computation.14 | async-start | bytes 7077888 | tf_op jit(solution)/shard_map/all_gather | solution.py:102
  546.3 432.6 %all-gather.26.cloned.1.call-start = ((), (), s32[]{:S(2)}) async-start(), calls=%async_computation.15 | async-start | bytes 7077888 | tf_op jit(solution)/shard_map/all_gather | solution.py:103
  547.0 761.9 %all-reduce.78.cloned.1.call-start = ((), (), s32[]{:S(2)}) async-start(), calls=%async_computation.17 | async-start | bytes 16777216 | tf_op jit(solution)/shard_map/psum | solution.py:198
  559.3 749.6 %copy-start.40 = (f32[4,1,512]{2,1,0:T(1,128)}, f32[4,1,512]{2,1,0:T(1,128)S(1)}, u32[]{:S(2)}) copy-start(f32[4,1,512]{2,1,0:T(1,128)S(1)} %convert_element_type.181) | copy-start | bytes 24580
  842.3 466.7 %copy-start.47 = (f32[1024]{0:T(1024)}, f32[1024]{0:T(1024)S(1)}, u32[]{:S(2)}) copy-start(f32[1024]{0:T(1024)S(1)} %fusion.101) | copy-start | bytes 12292
  997.4 10.0 copy-start.108
  997.4 10.0 copy-start.101
  1018.0 820.8 %all-reduce.80.cloned.1.call-start = ((), (), s32[]{:S(2)}) async-start(), calls=%async_computation.25 | async-start | bytes 2883584 | tf_op jit(solution)/shard_map/psum | solution.py:303
  1308.9 8.4 copy-start.9
  1309.0 9.4 copy-start.30
  1323.3 11.8 copy-start.15
  1472.1 21.0 copy-start.62
  1472.1 21.0 copy-start.63
  1519.4 30.4 %copy-start.60 = (f32[4,1,704]{2,1,0:T(1,128)S(1)}, f32[4,1,704]{2,1,0:T(1,128)}, u32[]{:S(2)}) copy-start(f32[4,1,704]{2,1,0:T(1,128)} %slice.804) | copy-start | bytes 33796
  1527.6 30.1 %copy-start.59 = (f32[4,1,704]{2,1,0:T(1,128)S(1)}, f32[4,1,704]{2,1,0:T(1,128)}, u32[]{:S(2)}) copy-start(f32[4,1,704]{2,1,0:T(1,128)} %slice.829) | copy-start | bytes 33796
  1563.1 10.0 copy-start.65
  1570.6 15.6 copy-start.64
  1678.3 22.2 copy-start.37
  1678.3 24.5 copy-start.21
  1718.4 25.0 copy-start.5
  1718.4 25.0 copy-start.42
  1718.4 25.0 copy-start.44
  1718.4 25.0 copy-start.50
  1718.4 25.0 copy-start.53
  1718.4 25.0 copy-start.54
  1774.3 8.7 copy-start.8
  1785.8 187.7 %reduce-scatter.9.cloned.1.call-start = ((), (), s32[]{:S(2)}) async-start(), calls=%async_computation.16 | async-start | bytes 10485760 | tf_op jit(solution)/shard_map/reduce_scatter | solution.py:187
  1797.6 323.4 %reduce-scatter.11.cloned.1.call-start = ((), (), s32[]{:S(2)}) async-start(), calls=%async_computation.18 | async-start | bytes 10485760 | tf_op jit(solution)/shard_map/reduce_scatter | solution.py:277
  1811.5 11.9 copy-start.103
  1811.5 11.9 copy-start.106
  1822.1 5.0 collective-permute-start.1
  1838.7 334.2 %all-reduce.82.cloned.1.call-start = ((), (), s32[]{:S(2)}) async-start(), calls=%async_computation.26 | async-start | bytes 2883584 | tf_op jit(solution)/shard_map/psum | solution.py:302
  1839.4 396.8 %reduce-scatter.17.cloned.1.call-start = ((), (), s32[]{:S(2)}) async-start(), calls=%async_computation.21 | async-start | bytes 6488064 | tf_op jit(solution)/shard_map/reduce_scatter | solution.py:287
  1848.3 450.9 %reduce-scatter.13.cloned.1.call-start = ((), (), s32[]{:S(2)}) async-start(), calls=%async_computation.19 | async-start | bytes 6488064 | tf_op jit(solution)/shard_map/reduce_scatter | solution.py:285
  1856.7 505.8 %reduce-scatter.15.cloned.1.call-start = ((), (), s32[]{:S(2)}) async-start(), calls=%async_computation.20 | async-start | bytes 6488064 | tf_op jit(solution)/shard_map/reduce_scatter | solution.py:286
  1865.5 593.3 %reduce-scatter.19.cloned.1.call-start = ((), (), s32[]{:S(2)}) async-start(), calls=%async_computation.22 | async-start | bytes 14155776 | tf_op jit(solution)/shard_map/reduce_scatter | solution.py:288
  1878.2 676.9 %reduce-scatter.21.cloned.1.call-start = ((), (), s32[]{:S(2)}) async-start(), calls=%async_computation.23 | async-start | bytes 14155776 | tf_op jit(solution)/shard_map/reduce_scatter | solution.py:289
  1890.8 760.8 %reduce-scatter.23.cloned.1.call-start = ((), (), s32[]{:S(2)}) async-start(), calls=%async_computation.24 | async-start | bytes 14155776 | tf_op jit(solution)/shard_map/reduce_scatter | solution.py:290
  1903.4 13.2 copy-start.91
  1903.4 13.2 copy-start.92
  1903.5 13.2 copy-start.93
  (66 other events, 227.3 us)
Sparse Core Ops, SparseCore 0:
  9.6 83.4 all-gather.13
  95.0 30.1 all-gather.15
  127.1 31.8 all-gather.17
  160.7 31.6 all-gather.19
  545.1 291.4 all-reduce.75
  838.3 44.5 all-gather.21
  884.7 45.5 all-gather.23
  932.1 46.6 all-gather.25
  1018.1 290.8 all-reduce.77
  1785.9 39.9 all-reduce.79
  1828.3 145.1 reduce-scatter.8
  1975.7 145.2 reduce-scatter.10
  2123.3 49.5 all-reduce.81
  2177.2 59.0 reduce-scatter.16
  2240.1 58.9 reduce-scatter.12
  2303.4 59.0 reduce-scatter.14
  2366.4 92.3 reduce-scatter.18
  2462.7 92.3 reduce-scatter.20
  2559.2 92.3 reduce-scatter.22
